TPU v7x, 32 devices: a whole 2x2x4 slice. The times are simulated.
32 devices in a mesh: space: 16 (over z, x, core), mem: 2 (over y).
Axes of the slice: x: 2, y: 2, z: 4, core: 2. Of those that a mesh axis runs over, the one named last changes fastest.
Arguments:
- ensemble: bfloat16 [8, 32, 512, 1536], P('mem', None, 'space'), may hold values from -12 to 12
- vector: bfloat16 [32, 512, 1536], P(None, 'space'), may hold values from -6 to 6
- modes: float32 [16, 32], replicated, may hold values from -1 to 1
- legendre: bfloat16 [512, 512, 256], P('space'), may hold values from -0.25 to 0.25
- spectrum: float32 [512, 256], P('space'), may hold values from 0.1 to 1
- truncation: int32 [1], replicated, may hold values from 543 to 702
Outputs:
- covariance_apply: bfloat16 [32, 512, 1536], P(None, 'space')
All inputs are finite; a program needn't handle non-finite values.
Results may differ from a plain program's by a relative error of at most 0.014.
Values may be sent and summed in bfloat16 or wider, within the bound.
A program may use at most 128 MiB of HBM per device.

v0:
```python
import math
import jax
import jax.numpy as jnp
from jax import lax
from jax.sharding import PartitionSpec as P

NMODE = 16
NLON = 1536
M = 512
NDEG = 256


def fourier_table(length, wave_count):
    points = jnp.arange(length, dtype=jnp.int32)
    orders = jnp.arange(wave_count, dtype=jnp.int32)
    phases = points[:, None] * orders[None, :] % length
    angles = phases.astype(jnp.float32) * (2.0 * math.pi / length)
    amplitude = math.sqrt(2.0 / length)
    stacked = jnp.stack([jnp.cos(angles), -jnp.sin(angles)], axis=-1) * amplitude
    return stacked.reshape(length, 2 * wave_count).astype(jnp.bfloat16)


def on_device(ensemble, vector, modes, legendre, spectrum, truncation):
    members = ensemble.shape[0]
    lat_rows = ensemble.shape[2]
    own_waves = legendre.shape[0]
    sources = lax.axis_size("space")
    total_members = members * lax.axis_size("mem")
    highest = lax.Precision.HIGHEST
    fourier = fourier_table(NLON, M)
    product = ensemble.astype(jnp.float32) * vector.astype(jnp.float32)[None]
    projected = jnp.einsum("jl,klac->kjac", modes, product, precision=highest).astype(jnp.bfloat16)
    fields = members * NMODE
    columns = fields * lat_rows
    zonal_parts = lax.dot_general(
        fourier,
        projected.reshape(columns, NLON),
        (((0,), (1,)), ((), ())),
        preferred_element_type=jnp.float32,
    )
    zonal_parts = zonal_parts.astype(jnp.bfloat16).reshape(1, 2 * M, columns)
    first_wave = lax.axis_index("space") * own_waves
    wavenumber = (
        first_wave
        + jnp.arange(own_waves, dtype=jnp.int32)[:, None]
        + jnp.arange(NDEG, dtype=jnp.int32)[None, :]
    )
    factor = jnp.where(wavenumber <= truncation[0], spectrum, jnp.zeros_like(spectrum))
    arrived = lax.all_to_all(zonal_parts, "space", split_axis=1, concat_axis=0, tiled=True)
    arrived = arrived.reshape(sources, own_waves, 2, fields, lat_rows)
    legendre_view = legendre.reshape(own_waves, sources, lat_rows, NDEG)
    harmonic = jnp.einsum(
        "smrfa,msan->mrfn", arrived, legendre_view, preferred_element_type=jnp.float32
    )
    weighted = (harmonic * factor[:, None, None, :]).astype(jnp.bfloat16)
    synthesis = jnp.einsum(
        "mrfn,msan->smrfa", weighted, legendre_view, preferred_element_type=jnp.float32
    )
    synthesis = synthesis.astype(jnp.bfloat16).reshape(sources, 2 * own_waves, columns)
    returned = lax.all_to_all(synthesis, "space", split_axis=0, concat_axis=1, tiled=True)
    spread = lax.dot_general(
        returned.reshape(2 * M, columns),
        fourier,
        (((0,), (1,)), ((), ())),
        preferred_element_type=jnp.float32,
    )
    spread = spread.reshape(members, NMODE, lat_rows, NLON)
    lifted = jnp.einsum("jl,kjac->klac", modes, spread, precision=highest)
    partial_value = jnp.sum(ensemble.astype(jnp.float32) * lifted, axis=0)
    summed = lax.psum(partial_value.astype(jnp.bfloat16), "mem").astype(jnp.float32)
    return (summed / (total_members - 1)).astype(jnp.bfloat16)


def solution(mesh):
    placed = (
        P("mem", None, "space", None),
        P(None, "space", None),
        P(),
        P("space", None, None),
        P("space", None),
        P(),
    )
    return jax.shard_map(
        on_device, mesh=mesh, in_specs=placed, out_specs=P(None, "space", None), check_vma=False
    )
```

profile of v0, /device:TPU:0, one launch (start us, length us, event | category | flops | bytes accessed | tf_op | source)
XLA Modules:
  0.0 595.8 jit_solution(11271373535638854482)
XLA Ops:
  6.5 12.9 %sine_negate_fusion = (f32[1536,512,1]{1,0,2:T(8,128)S(1)}, f32[1536,512,1]{1,0,2:T(8,128)S(1)}) fusion(), kind=kLoop, calls=%fused_computation.23 | loop fusion | flops 7864320 | bytes 6291456 | tf_op jit(solution)/shard_map/neg | solution.py:19
  21.3 19.5 %convert_bitcast_fusion.1 = bf16[4,16,32,1536]{3,1,2,0:T(8,128)(2,1)S(1)} fusion(f32[32,32,1536]{2,0,1:T(8,128)S(1)} %copy.28, bf16[4,32,32,1536]{3,2,1,0:T(8,128)(2,1)S(1)} %copy-done.1, f32[16,32]{1,0:T(8,128)S(1)} %copy-done), kind=kOutput, calls=%fused_computation.13 | convolution fusion | flops 1223688192 | bytes 25167872 | tf_op jit(solution)/shard_map/jl,klac->kjac/dot_general | solution.py:32
  40.8 6.1 %copy.29 = bf16[4,16,32,1536]{3,2,1,0:T(8,128)(2,1)} copy(bf16[4,16,32,1536]{3,1,2,0:T(8,128)(2,1)S(1)} %convert_bitcast_fusion.1) | data formatting | bytes 12582912 | tf_op jit(solution)/shard_map/convert_element_type | solution.py:32
  49.5 7.4 %copy.27 = bf16[1536,512,2]{0,2,1:T(2,128)(2,1)S(1)} copy(bf16[1536,512,2]{1,0,2:T(8,128)(2,1)} %fusion.7) | data formatting | bytes 6291456 | tf_op jit(solution)/shard_map/convert_element_type | solution.py:20
  59.6 10.0 %convert_bitcast_fusion.2 = bf16[1,1024,2048]{2,1,0:T(8,128)(2,1)S(1)} fusion(bf16[1536,1024]{0,1:T(8,128)(2,1)} %convert_element_type.69, bf16[2048,1536]{1,0:T(8,128)(2,1)} %bitcast.60), kind=kOutput, calls=%fused_computation.19 | convolution fusion | flops 6444548096 | bytes 13631488 | tf_op jit(solution)/shard_map/dot_general | solution.py:35
  69.6 24.6 %copy.67 = bf16[1,1024,2048]{2,0,1:T(2,128)(2,1)} copy(bf16[1,1024,2048]{2,1,0:T(8,128)(2,1)S(1)} %convert_bitcast_fusion.2) | data formatting | bytes 8388608 | tf_op jit(solution)/shard_map/reshape | solution.py:41
  94.8 27.4 %reduce.2 = bf16[1024,2048]{1,0:T(8,128)(2,1)} reduce(bf16[1024,1,2048]{2,1,0:T(2,128)(2,1)} %bitcast.56, bf16[]{:T(256)} %broadcast.88), dimensions={1}, to_apply=%bitcast.54.reduce_sub_computation | reduce | bytes 8388610
  122.1 11.4 %reshape.117 = bf16[16,2,65536]{2,1,0:T(2,128)(2,1)} reshape(bf16[1024,2048]{1,0:T(8,128)(2,1)} %reduce.2) | data formatting | bytes 8388608
  133.5 7.6 %all-to-all-start = ((bf16[16,2,65536]{2,1,0:T(2,128)(2,1)}), bf16[16,2,65536]{2,1,0:T(2,128)(2,1)}, u32[]{:S(2)}, u32[]{:S(2)}) async-start(bf16[16,2,65536]{2,1,0:T(2,128)(2,1)} %reshape.117), calls=%async_computation | async-start | bytes 8388608 | tf_op jit(solution)/shard_map/all_to_all | solution.py:49
  141.9 76.7 %all-to-all-done = bf16[16,2,65536]{2,1,0:T(2,128)(2,1)} async-done(((bf16[16,2,65536]{2,1,0:T(2,128)(2,1)}), bf16[16,2,65536]{2,1,0:T(2,128)(2,1)}, u32[]{:S(2)}, u32[]{:S(2)}) %all-to-all-start) | async-done | bytes 4194336 | tf_op jit(solution)/shard_map/all_to_all | solution.py:49
  218.6 12.7 %reshape.118 = bf16[1024,1,2048]{2,1,0:T(2,128)(2,1)} reshape(bf16[16,2,65536]{2,1,0:T(2,128)(2,1)} %all-to-all-done) | data formatting | bytes 8388608
  231.3 27.3 %bitcast_reduce_fusion = bf16[1024,2048]{1,0:T(8,128)(2,1)} fusion(bf16[1024,1,2048]{2,1,0:T(2,128)(2,1)} %reshape.118), kind=kLoop, calls=%fused_computation.36 | loop fusion | bytes 8388608 | tf_op jit(solution)/shard_map/all_to_all | solution.py:49
  258.6 19.5 %reshape.106 = bf16[16,32,2,64,32]{4,3,2,1,0:T(8,128)(2,1)} reshape(bf16[1024,2048]{1,0:T(8,128)(2,1)} %bitcast_reduce_fusion) | data formatting | bytes 8388608 | tf_op jit(solution)/shard_map/reshape | solution.py:50
  278.1 10.1 %fusion.2 = f32[32,2,64,256,1]{3,2,0,1,4:T(8,128)S(1)} fusion(bf16[16,32,2,64,32]{4,3,2,1,0:T(8,128)(2,1)} %reshape.106, bf16[32,16,32,256,1]{3,2,1,0,4:T(8,128)(2,1)} %bitcast.58), kind=kOutput, calls=%fused_computation.4 | convolution fusion | flops 1073741824 | bytes 16777216 | tf_op jit(solution)/shard_map/smrfa,msan->mrfn/dot_general | solution.py:52
  288.2 10.0 %convert_bitcast_fusion = bf16[16,32,2,64,32]{3,4,0,2,1:T(8,128)(2,1)} fusion(bf16[32,16,32,256,1]{3,2,1,4,0:T(8,128)(2,1)} %bitcast.59, f32[32,2,64,256,1]{3,2,0,1,4:T(8,128)S(1)} %fusion.2, f32[32,256]{1,0:T(8,128)S(1)} %fusion.21), kind=kOutput, calls=%fused_computation.9 | convolution fusion | flops 1077936128 | bytes 16809984 | tf_op jit(solution)/shard_map/mrfn,msan->smrfa/dot_general | solution.py:56
  298.3 15.9 %copy.33 = bf16[16,32,2,64,32]{4,3,2,1,0:T(8,128)(2,1)} copy(bf16[16,32,2,64,32]{3,4,0,2,1:T(8,128)(2,1)} %convert_bitcast_fusion) | data formatting | bytes 8388608 | tf_op jit(solution)/shard_map/convert_element_type | solution.py:59
  314.2 22.6 %reshape.108 = bf16[16,64,2048]{2,1,0:T(8,128)(2,1)} reshape(bf16[16,32,2,64,32]{4,3,2,1,0:T(8,128)(2,1)} %copy.33) | data formatting | bytes 8388608 | tf_op jit(solution)/shard_map/reshape | solution.py:59
  336.7 112.0 %all_to_all.8 = bf16[16,64,2048]{2,1,0:T(8,128)(2,1)} all-to-all(bf16[16,64,2048]{2,1,0:T(8,128)(2,1)} %reshape.108), channel_id=1, replica_groups=mesh['space'=16,'mem'=2] {'space'}, dimensions={0} | all-to-all | bytes 8388608 | tf_op jit(solution)/shard_map/all_to_all | solution.py:60
  448.8 6.6 %copy.34 = bf16[1024,2048]{0,1:T(8,128)(2,1)} copy(bf16[1024,2048]{1,0:T(8,128)(2,1)} %bitcast.57) | data formatting | bytes 8388608 | tf_op jit(solution)/shard_map/reshape | solution.py:62
  455.3 9.5 %fusion.9 = f32[4,16,32,1536]{3,1,2,0:T(8,128)S(1)} fusion(bf16[4,16,32,1024]{3,2,1,0:T(8,128)(2,1)} %bitcast.61, bf16[1536,1024]{0,1:T(8,128)(2,1)S(1)} %copy-done.2), kind=kOutput, calls=%fused_computation.17 | convolution fusion | flops 6442450944 | bytes 19922944 | tf_op jit(solution)/shard_map/dot_general | solution.py:61
  464.8 31.1 %fusion.1 = bf16[32,32,1536]{2,0,1:T(8,128)(2,1)} fusion(f32[4,16,32,1536]{3,1,2,0:T(8,128)S(1)} %fusion.9, bf16[4,32,32,1536]{3,2,1,0:T(8,128)(2,1)} %param.6, f32[16,32]{1,0:T(8,128)S(1)} %copy-done), kind=kOutput, calls=%fused_computation.3 | convolution fusion | flops 1225261056 | bytes 28313600 | tf_op jit(solution)/shard_map/jl,kjac->klac/dot_general | solution.py:68
  496.0 86.7 %all-reduce.2.cloned.1.call-done = bf16[32,32,1536]{2,0,1:T(8,128)(2,1)} async-done(((bf16[32,32,1536]{2,0,1:T(8,128)(2,1)}), bf16[32,32,1536]{2,0,1:T(8,128)(2,1)}) %all-reduce.2.cloned.1.call-update) | async-done | bytes 3145744 | tf_op jit(solution)/shard_map/psum | solution.py:70
  582.6 2.7 multiply_convert_fusion
  585.3 3.4 copy.37
  (18 shorter events, 7.7 us)
Async XLA Ops:
  6.5 14.8 %copy-start = (f32[16,32]{1,0:T(8,128)S(1)}, f32[16,32]{1,0:T(8,128)}, u32[]{:S(2)}) copy-start(f32[16,32]{1,0:T(8,128)} %param.8) | copy-start | bytes 6148
  6.5 12.9 %copy-start.3 = (bf16[32,32,1536]{2,1,0:T(8,128)(2,1)S(1)}, bf16[32,32,1536]{2,1,0:T(8,128)(2,1)}, u32[]{:S(2)}) copy-start(bf16[32,32,1536]{2,1,0:T(8,128)(2,1)} %param.7) | copy-start | bytes 9437188
  6.5 14.8 %copy-start.1 = (bf16[4,32,32,1536]{3,2,1,0:T(8,128)(2,1)S(1)}, bf16[4,32,32,1536]{3,2,1,0:T(8,128)(2,1)}, u32[]{:S(2)}) copy-start(bf16[4,32,32,1536]{3,2,1,0:T(8,128)(2,1)} %param.6) | copy-start | bytes 37748740
  133.5 8.3 %copy-start.4 = (f32[32,256]{1,0:T(8,128)S(1)}, f32[32,256]{1,0:T(8,128)}, u32[]{:S(2)}) copy-start(f32[32,256]{1,0:T(8,128)} %param.10) | copy-start | bytes 98308
  133.5 85.1 %all-to-all-start = ((bf16[16,2,65536]{2,1,0:T(2,128)(2,1)}), bf16[16,2,65536]{2,1,0:T(2,128)(2,1)}, u32[]{:S(2)}, u32[]{:S(2)}) async-start(bf16[16,2,65536]{2,1,0:T(2,128)(2,1)} %reshape.117), calls=%async_computation | async-start | bytes 8388608 | tf_op jit(solution)/shard_map/all_to_all | solution.py:49
  141.1 441.5 %all-reduce.2.cloned.1.call-start = ((), (), s32[]{:S(2)}) async-start(), calls=%async_computation.2 | async-start | bytes 6291456 | tf_op jit(solution)/shard_map/psum | solution.py:70
  448.8 6.6 %copy-start.2 = (bf16[1536,1024]{0,1:T(8,128)(2,1)S(1)}, bf16[1536,1024]{0,1:T(8,128)(2,1)}, u32[]{:S(2)}) copy-start(bf16[1536,1024]{0,1:T(8,128)(2,1)} %convert_element_type.69) | copy-start | bytes 9437188
Sparse Core Ops, SparseCore 0:
  496.1 86.5 all-reduce.1
where the time goes:
time: 607 us; the launch traced here: 596 us
  local copies, waits for them, and re-layouts  163 us (27%)
  waiting for transfers between devices  163 us (27%)
  blocking collectives  112 us (18%)
  matrix products  90.2 us (15%)
  other arithmetic  45.6 us (8%)
  between operations  14.4 us (2%)
  starting transfers between devices  7.61 us (1%)
    all_to_all x1, blocking collectives, on_device(): lax.all_to_all(synthesis, 'space', split_axis=0, concat_axis=1, tiled=True)  112 us
    psum x1, waiting for transfers between devices, on_device(): lax.psum(partial_value.astype(jnp.bfloat16), 'mem').astype(jnp.float32)  86.7 us
    all_to_all x1, waiting for transfers between devices, on_device(): lax.all_to_all(zonal_parts, 'space', split_axis=1, concat_axis=0, tiled=T...  76.7 us
    dot_general x1, matrix products, on_device(): lifted = jnp.einsum('jl,kjac->klac', modes, spread, precision=highest)  31.1 us
    unnamed x1, other arithmetic  27.4 us
    all_to_all x1, local copies, waits for them, and re-layouts, on_device(): lax.all_to_all(zonal_parts, 'space', split_axis=1, concat_axis=0, tiled=T...  27.3 us
    reshape x1, local copies, waits for them, and re-layouts, on_device(): zonal_parts = zonal_parts.astype(jnp.bfloat16).reshape(1, 2 * M, columns)  24.6 us
    unnamed x13, local copies, waits for them, and re-layouts  24.6 us
  transfers between devices with their start and end apart: 2, of which 2 were waited for; matrix products, arithmetic and copies ran while one was open for 0% of the time, Pallas kernels for 0%

commit v1 on v0

--- a/solution.py
+++ b/solution.py
@@ -3,11 +3,20 @@
 import jax.numpy as jnp
 from jax import lax
 from jax.sharding import PartitionSpec as P
+from jax.lax import all_to_all, axis_size
 
 NMODE = 16
 NLON = 1536
 M = 512
 NDEG = 256
+
+
+def supply_racks(array_dim, arr, join_dim):
+    formed = axis_size("space")
+    u_next = jnp.stack(jnp.split(arr, formed, axis=array_dim))
+    z = all_to_all(u_next, "space", 0, 0)
+    n_now = jnp.concatenate(z, axis=join_dim)
+    return n_now
 
 
 def fourier_table(length, wave_count):
@@ -57,7 +66,7 @@
         "mrfn,msan->smrfa", weighted, legendre_view, preferred_element_type=jnp.float32
     )
     synthesis = synthesis.astype(jnp.bfloat16).reshape(sources, 2 * own_waves, columns)
-    returned = lax.all_to_all(synthesis, "space", split_axis=0, concat_axis=1, tiled=True)
+    returned = supply_racks(0, arr=synthesis, join_dim=1)
     spread = lax.dot_general(
         returned.reshape(2 * M, columns),
         fourier,

time: 607 us -> 636 us (1.048)
  local copies, waits for them, and re-layouts: 163 us -> 190 us
    another operation x0 -> x18, local copies, waits for them, and re-layouts: none -> 36.3 us  [the longest x17 29.8 us: supply_racks(): u_next = jnp.stack(jnp.split(arr, formed, axis=array_dim))]
    reshape x2 -> x0, local copies, waits for them, and re-layouts: 29.1 us -> none  [the longest x1 22.6 us: on_device(): synthesis.astype(jnp.bfloat16).reshape(sources, 2 * own_waves, columns)]
    split x0 -> x17, local copies, waits for them, and re-layouts: none -> 26.3 us  [supply_racks(): u_next = jnp.stack(jnp.split(arr, formed, axis=array_dim))]
    convert_element_type x1 -> x0, local copies, waits for them, and re-layouts: 15.9 us -> none  [on_device(): synthesis.astype(jnp.bfloat16).reshape(sources, 2 * own_waves, columns)]
    unnamed x13 -> x54, local copies, waits for them, and re-layouts: 24.6 us -> 35.5 us
where the time goes in v1:
time: 636 us; the launch traced here: 625 us
  local copies, waits for them, and re-layouts  190 us (30%)
  waiting for transfers between devices  163 us (26%)
  blocking collectives  112 us (18%)
  matrix products  91.3 us (14%)
  other arithmetic  45.6 us (7%)
  between operations  14.6 us (2%)
  starting transfers between devices  7.61 us (1%)
    all_to_all x1, blocking collectives, supply_racks(): z = all_to_all(u_next, 'space', 0, 0)  112 us
    psum x1, waiting for transfers between devices, on_device(): lax.psum(partial_value.astype(jnp.bfloat16), 'mem').astype(jnp.float32)  86.7 us
    all_to_all x1, waiting for transfers between devices, on_device(): lax.all_to_all(zonal_parts, 'space', split_axis=1, concat_axis=0, tiled=T...  76.7 us
    unnamed x54, local copies, waits for them, and re-layouts  35.5 us
    dot_general x1, matrix products, on_device(): lifted = jnp.einsum('jl,kjac->klac', modes, spread, precision=highest)  31 us
    another operation x17, local copies, waits for them, and re-layouts, supply_racks(): u_next = jnp.stack(jnp.split(arr, formed, axis=array_dim))  29.8 us
    unnamed x1, other arithmetic  27.4 us
    all_to_all x1, local copies, waits for them, and re-layouts, on_device(): lax.all_to_all(zonal_parts, 'space', split_axis=1, concat_axis=0, tiled=T...  27.3 us
  transfers between devices with their start and end apart: 2, of which 2 were waited for; matrix products, arithmetic and copies ran while one was open for 0% of the time, Pallas kernels for 0%

profile of v1, /device:TPU:0, one launch (start us, length us, event | category | flops | bytes accessed | tf_op | source)
XLA Modules:
  0.0 625.1 jit_solution(16767676550870740987)
XLA Ops:
  6.5 12.9 %sine_negate_fusion = (f32[1536,512,1]{1,0,2:T(8,128)S(1)}, f32[1536,512,1]{1,0,2:T(8,128)S(1)}) fusion(), kind=kLoop, calls=%fused_computation.23 | loop fusion | flops 7864320 | bytes 6291456 | tf_op jit(solution)/shard_map/neg | solution.py:28
  22.0 7.4 %copy.57 = bf16[1536,512,2]{0,2,1:T(2,128)(2,1)S(1)} copy(bf16[1536,512,2]{1,0,2:T(8,128)(2,1)} %fusion.7) | data formatting | bytes 6291456 | tf_op jit(solution)/shard_map/convert_element_type | solution.py:29
  32.1 3.7 copy.58
  35.9 23.7 %convert_bitcast_fusion.1 = bf16[4,16,32,1536]{3,1,2,0:T(8,128)(2,1)S(1)} fusion(f32[32,32,1536]{2,0,1:T(8,128)S(1)} %copy.58, bf16[4,32,32,1536]{3,2,1,0:T(8,128)(2,1)} %param.6, f32[16,32]{1,0:T(8,128)S(1)} %copy-done), kind=kOutput, calls=%fused_computation.13 | convolution fusion | flops 1223688192 | bytes 25167872 | tf_op jit(solution)/shard_map/jl,klac->kjac/dot_general | solution.py:41
  59.5 3.5 copy.59
  63.1 6.9 %convert_bitcast_fusion.2 = bf16[1,1024,2048]{2,1,0:T(8,128)(2,1)S(1)} fusion(bf16[1536,1024]{0,1:T(8,128)(2,1)S(1)} %copy-done.1, bf16[2048,1536]{1,0:T(8,128)(2,1)S(1)} %bitcast.90), kind=kOutput, calls=%fused_computation.19 | convolution fusion | flops 6444548096 | bytes 13631488 | tf_op jit(solution)/shard_map/dot_general | solution.py:44
  70.0 24.7 %copy.112 = bf16[1,1024,2048]{2,0,1:T(2,128)(2,1)} copy(bf16[1,1024,2048]{2,1,0:T(8,128)(2,1)S(1)} %convert_bitcast_fusion.2) | data formatting | bytes 8388608 | tf_op jit(solution)/shard_map/reshape | solution.py:50
  95.2 27.4 %reduce.2 = bf16[1024,2048]{1,0:T(8,128)(2,1)} reduce(bf16[1024,1,2048]{2,1,0:T(2,128)(2,1)} %bitcast.86, bf16[]{:T(256)} %broadcast.88), dimensions={1}, to_apply=%bitcast.84.reduce_sub_computation | reduce | bytes 8388610
  122.6 11.4 %reshape.138 = bf16[16,2,65536]{2,1,0:T(2,128)(2,1)} reshape(bf16[1024,2048]{1,0:T(8,128)(2,1)} %reduce.2) | data formatting | bytes 8388608
  133.9 7.6 %all-to-all-start = ((bf16[16,2,65536]{2,1,0:T(2,128)(2,1)}), bf16[16,2,65536]{2,1,0:T(2,128)(2,1)}, u32[]{:S(2)}, u32[]{:S(2)}) async-start(bf16[16,2,65536]{2,1,0:T(2,128)(2,1)} %reshape.138), calls=%async_computation | async-start | bytes 8388608 | tf_op jit(solution)/shard_map/all_to_all | solution.py:58
  142.3 76.7 %all-to-all-done = bf16[16,2,65536]{2,1,0:T(2,128)(2,1)} async-done(((bf16[16,2,65536]{2,1,0:T(2,128)(2,1)}), bf16[16,2,65536]{2,1,0:T(2,128)(2,1)}, u32[]{:S(2)}, u32[]{:S(2)}) %all-to-all-start) | async-done | bytes 4194336 | tf_op jit(solution)/shard_map/all_to_all | solution.py:58
  219.0 12.7 %reshape.139 = bf16[1024,1,2048]{2,1,0:T(2,128)(2,1)} reshape(bf16[16,2,65536]{2,1,0:T(2,128)(2,1)} %all-to-all-done) | data formatting | bytes 8388608
  231.8 27.3 %bitcast_reduce_fusion = bf16[1024,2048]{1,0:T(8,128)(2,1)} fusion(bf16[1024,1,2048]{2,1,0:T(2,128)(2,1)} %reshape.139), kind=kLoop, calls=%fused_computation.53 | loop fusion | bytes 8388608 | tf_op jit(solution)/shard_map/all_to_all | solution.py:58
  259.1 19.5 %reshape.129 = bf16[16,32,2,64,32]{4,3,2,1,0:T(8,128)(2,1)} reshape(bf16[1024,2048]{1,0:T(8,128)(2,1)} %bitcast_reduce_fusion) | data formatting | bytes 8388608 | tf_op jit(solution)/shard_map/reshape | solution.py:59
  278.5 10.1 %fusion.2 = f32[32,2,64,256,1]{3,2,0,1,4:T(8,128)S(1)} fusion(bf16[16,32,2,64,32]{4,3,2,1,0:T(8,128)(2,1)} %reshape.129, bf16[32,16,32,256,1]{3,2,1,0,4:T(8,128)(2,1)} %bitcast.88), kind=kOutput, calls=%fused_computation.4 | convolution fusion | flops 1073741824 | bytes 16777216 | tf_op jit(solution)/shard_map/smrfa,msan->mrfn/dot_general | solution.py:61
  288.6 10.1 %convert_bitcast_fusion = bf16[16,32,2,64,32]{3,4,0,2,1:T(8,128)(2,1)} fusion(bf16[32,16,32,256,1]{3,2,1,4,0:T(8,128)(2,1)} %bitcast.89, f32[32,2,64,256,1]{3,2,0,1,4:T(8,128)S(1)} %fusion.2, f32[32,256]{1,0:T(8,128)S(1)} %fusion.21), kind=kOutput, calls=%fused_computation.9 | convolution fusion | flops 1077936128 | bytes 16809984 | tf_op jit(solution)/shard_map/mrfn,msan->smrfa/dot_general | solution.py:65
  298.7 6.3 %fusion.24 = (bf16[1,32,2,64,32]{3,4,0,2,1:T(8,128)(2,1)S(1)}, bf16[1,32,2,64,32]{3,4,0,2,1:T(8,128)(2,1)S(1)}, bf16[1,32,2,64,32]{3,4,0,2,1:T(8,128)(2,1)S(1)},...) fusion(bf16[16,32,2,64,32]{3,4,0,2,1:T(8,128)(2,1)} %convert_bi, ...), kind=kLoop, calls=%fused_computation.52 | loop fusion | bytes 8388608 | tf_op jit(solution)/shard_map/split | solution.py:16
  365.9 112.3 %all_to_all.14 = bf16[16,1,64,2048]{3,2,1,0:T(8,128)(2,1)} all-to-all(bf16[16,1,64,2048]{3,2,1,0:T(8,128)(2,1)} %constant_dynamic-update-slice_fusion), channel_id=1, replica_groups=mesh['space'=16,'mem'=2] {'space'}, dimensions={0} | all-to-all | bytes 8388608 | tf_op jit(solution)/shard_map/all_to_all | solution.py:17
  478.1 6.6 %copy.79 = bf16[1024,2048]{0,1:T(8,128)(2,1)} copy(bf16[1024,2048]{1,0:T(8,128)(2,1)} %bitcast.87) | data formatting | bytes 8388608 | tf_op jit(solution)/shard_map/reshape;reshape | solution.py:71
  484.7 9.5 %fusion.9 = f32[4,16,32,1536]{3,1,2,0:T(8,128)S(1)} fusion(bf16[4,16,32,1024]{3,2,1,0:T(8,128)(2,1)} %bitcast.91, bf16[1536,1024]{0,1:T(8,128)(2,1)S(1)} %copy-done.2), kind=kOutput, calls=%fused_computation.17 | convolution fusion | flops 6442450944 | bytes 19922944 | tf_op jit(solution)/shard_map/dot_general | solution.py:70
  494.2 31.0 %fusion.1 = bf16[32,32,1536]{2,0,1:T(8,128)(2,1)} fusion(f32[4,16,32,1536]{3,1,2,0:T(8,128)S(1)} %fusion.9, bf16[4,32,32,1536]{3,2,1,0:T(8,128)(2,1)} %param.6, f32[16,32]{1,0:T(8,128)S(1)} %copy-done), kind=kOutput, calls=%fused_computation.3 | convolution fusion | flops 1225261056 | bytes 28313600 | tf_op jit(solution)/shard_map/jl,kjac->klac/dot_general | solution.py:77
  525.3 86.7 %all-reduce.2.cloned.1.call-done = bf16[32,32,1536]{2,0,1:T(8,128)(2,1)} async-done(((bf16[32,32,1536]{2,0,1:T(8,128)(2,1)}), bf16[32,32,1536]{2,0,1:T(8,128)(2,1)}) %all-reduce.2.cloned.1.call-update) | async-done | bytes 3145744 | tf_op jit(solution)/shard_map/psum | solution.py:79
  612.0 2.7 multiply_convert_fusion
  614.6 3.4 copy.82
  (91 shorter events, 66.5 us)
Async XLA Ops:
  6.5 29.3 %copy-start = (f32[16,32]{1,0:T(8,128)S(1)}, f32[16,32]{1,0:T(8,128)}, u32[]{:S(2)}) copy-start(f32[16,32]{1,0:T(8,128)} %param.8) | copy-start | bytes 6148
  59.5 3.5 copy-start.1
  133.9 8.3 %copy-start.17 = (f32[32,256]{1,0:T(8,128)S(1)}, f32[32,256]{1,0:T(8,128)}, u32[]{:S(2)}) copy-start(f32[32,256]{1,0:T(8,128)} %param.10) | copy-start | bytes 98308
  133.9 85.1 %all-to-all-start = ((bf16[16,2,65536]{2,1,0:T(2,128)(2,1)}), bf16[16,2,65536]{2,1,0:T(2,128)(2,1)}, u32[]{:S(2)}, u32[]{:S(2)}) async-start(bf16[16,2,65536]{2,1,0:T(2,128)(2,1)} %reshape.138), calls=%async_computation | async-start | bytes 8388608 | tf_op jit(solution)/shard_map/all_to_all | solution.py:58
  141.5 470.5 %all-reduce.2.cloned.1.call-start = ((), (), s32[]{:S(2)}) async-start(), calls=%async_computation.2 | async-start | bytes 6291456 | tf_op jit(solution)/shard_map/psum | solution.py:79
  348.2 7.5 %copy-start.3 = (bf16[1,1,64,2048]{3,2,1,0:T(8,128)(2,1)S(1)}, bf16[1,1,64,2048]{3,2,1,0:T(8,128)(2,1)}, u32[]{:S(2)}) copy-start(bf16[1,1,64,2048]{3,2,1,0:T(8,128)(2,1)} %stack.59) | copy-start | bytes 786436
  348.2 8.2 %copy-start.4 = (bf16[1,1,64,2048]{3,2,1,0:T(8,128)(2,1)S(1)}, bf16[1,1,64,2048]{3,2,1,0:T(8,128)(2,1)}, u32[]{:S(2)}) copy-start(bf16[1,1,64,2048]{3,2,1,0:T(8,128)(2,1)} %stack.60) | copy-start | bytes 786436
  348.2 8.9 %copy-start.5 = (bf16[1,1,64,2048]{3,2,1,0:T(8,128)(2,1)S(1)}, bf16[1,1,64,2048]{3,2,1,0:T(8,128)(2,1)}, u32[]{:S(2)}) copy-start(bf16[1,1,64,2048]{3,2,1,0:T(8,128)(2,1)} %stack.61) | copy-start | bytes 786436
  350.2 7.7 %copy-start.6 = (bf16[1,1,64,2048]{3,2,1,0:T(8,128)(2,1)S(1)}, bf16[1,1,64,2048]{3,2,1,0:T(8,128)(2,1)}, u32[]{:S(2)}) copy-start(bf16[1,1,64,2048]{3,2,1,0:T(8,128)(2,1)} %stack.62) | copy-start | bytes 786436
  350.6 8.0 %copy-start.7 = (bf16[1,1,64,2048]{3,2,1,0:T(8,128)(2,1)S(1)}, bf16[1,1,64,2048]{3,2,1,0:T(8,128)(2,1)}, u32[]{:S(2)}) copy-start(bf16[1,1,64,2048]{3,2,1,0:T(8,128)(2,1)} %stack.63) | copy-start | bytes 786436
  350.6 8.7 %copy-start.8 = (bf16[1,1,64,2048]{3,2,1,0:T(8,128)(2,1)S(1)}, bf16[1,1,64,2048]{3,2,1,0:T(8,128)(2,1)}, u32[]{:S(2)}) copy-start(bf16[1,1,64,2048]{3,2,1,0:T(8,128)(2,1)} %stack.64) | copy-start | bytes 786436
  353.0 7.0 %copy-start.9 = (bf16[1,1,64,2048]{3,2,1,0:T(8,128)(2,1)S(1)}, bf16[1,1,64,2048]{3,2,1,0:T(8,128)(2,1)}, u32[]{:S(2)}) copy-start(bf16[1,1,64,2048]{3,2,1,0:T(8,128)(2,1)} %stack.65) | copy-start | bytes 786436
  353.0 7.8 %copy-start.10 = (bf16[1,1,64,2048]{3,2,1,0:T(8,128)(2,1)S(1)}, bf16[1,1,64,2048]{3,2,1,0:T(8,128)(2,1)}, u32[]{:S(2)}) copy-start(bf16[1,1,64,2048]{3,2,1,0:T(8,128)(2,1)} %stack.66) | copy-start | bytes 786436
  354.9 6.6 %copy-start.11 = (bf16[1,1,64,2048]{3,2,1,0:T(8,128)(2,1)S(1)}, bf16[1,1,64,2048]{3,2,1,0:T(8,128)(2,1)}, u32[]{:S(2)}) copy-start(bf16[1,1,64,2048]{3,2,1,0:T(8,128)(2,1)} %stack.67) | copy-start | bytes 786436
  354.9 7.3 %copy-start.12 = (bf16[1,1,64,2048]{3,2,1,0:T(8,128)(2,1)S(1)}, bf16[1,1,64,2048]{3,2,1,0:T(8,128)(2,1)}, u32[]{:S(2)}) copy-start(bf16[1,1,64,2048]{3,2,1,0:T(8,128)(2,1)} %stack.68) | copy-start | bytes 786436
  354.9 8.0 %copy-start.13 = (bf16[1,1,64,2048]{3,2,1,0:T(8,128)(2,1)S(1)}, bf16[1,1,64,2048]{3,2,1,0:T(8,128)(2,1)}, u32[]{:S(2)}) copy-start(bf16[1,1,64,2048]{3,2,1,0:T(8,128)(2,1)} %stack.69) | copy-start | bytes 786436
  354.9 8.8 %copy-start.14 = (bf16[1,1,64,2048]{3,2,1,0:T(8,128)(2,1)S(1)}, bf16[1,1,64,2048]{3,2,1,0:T(8,128)(2,1)}, u32[]{:S(2)}) copy-start(bf16[1,1,64,2048]{3,2,1,0:T(8,128)(2,1)} %stack.70) | copy-start | bytes 786436
  355.0 9.5 %copy-start.15 = (bf16[1,1,64,2048]{3,2,1,0:T(8,128)(2,1)S(1)}, bf16[1,1,64,2048]{3,2,1,0:T(8,128)(2,1)}, u32[]{:S(2)}) copy-start(bf16[1,1,64,2048]{3,2,1,0:T(8,128)(2,1)} %stack.71) | copy-start | bytes 786436
  355.0 10.2 %copy-start.16 = (bf16[1,1,64,2048]{3,2,1,0:T(8,128)(2,1)S(1)}, bf16[1,1,64,2048]{3,2,1,0:T(8,128)(2,1)}, u32[]{:S(2)}) copy-start(bf16[1,1,64,2048]{3,2,1,0:T(8,128)(2,1)} %stack.72) | copy-start | bytes 786436
  478.1 6.6 %copy-start.2 = (bf16[1536,1024]{0,1:T(8,128)(2,1)S(1)}, bf16[1536,1024]{0,1:T(8,128)(2,1)}, u32[]{:S(2)}) copy-start(bf16[1536,1024]{0,1:T(8,128)(2,1)} %convert_element_type.69) | copy-start | bytes 9437188
Sparse Core Ops, SparseCore 0:
  525.4 86.5 all-reduce.1
